TPU v7x, 512 devices: a whole 4x8x8 slice. The times are simulated.
512 devices in a mesh: dp: 64 (over z_lo, y, x), seq: 8 (over z_hi, core).
Axes of the slice: x: 4, y: 8, z: 8 (z_hi: 4, z_lo: 2; z = z_hi * 2 + z_lo), core: 2. Of those that a mesh axis runs over, the one named last changes fastest.
Arguments:
- queries: bfloat16 [65536, 4096], P(('dp', 'seq')), may hold values from -48 to 48
- keys: bfloat16 [65536, 1024], P(('dp', 'seq')), may hold values from -6 to 6
- values: bfloat16 [65536, 1024], P(('dp', 'seq')), may hold values from -6 to 6
- out_grad: bfloat16 [65536, 4096], P(('dp', 'seq')), may hold values from -6 to 6
- normed: bfloat16 [65536, 4096], P(('dp', 'seq')), may hold values from -24 to 24
Outputs:
- query_grad: bfloat16 [65536, 4096], P(('dp', 'seq'))
- key_weight_grad: float32 [4096, 1024], P('dp', 'seq')
- value_weight_grad: float32 [4096, 1024], P('dp', 'seq')
All inputs are finite; a program needn't handle non-finite values.
Results may differ from a plain program's by a relative error of at most 0.0055.
Values may be sent and summed in bfloat16 or wider, within the bound.
A program may use at most 128 MiB of HBM per device.

v0:
```python
import math
import jax
import jax.numpy as jnp
from jax import lax
from jax.sharding import PartitionSpec as P

HD = 128


def unrotate(grad, position):
    half = HD // 2
    freqs = jnp.exp(-math.log(500000.0) * (2.0 * jnp.arange(half).astype(jnp.float32) / HD))
    angle = position.astype(jnp.float32)[:, None] * freqs[None, :]
    cosine = jnp.cos(angle)[:, None, :]
    sine = jnp.sin(angle)[:, None, :]
    first = grad[..., :half]
    second = grad[..., half:]
    return jnp.concatenate(
        [first * cosine + second * sine, second * cosine - first * sine], axis=-1
    )


def local(queries, keys, values, out_grad, normed):
    head_q, head_k, head_v, head_g = (
        lax.all_to_all(queries, "seq", split_axis=1, concat_axis=0, tiled=True),
        lax.all_to_all(keys, "seq", split_axis=1, concat_axis=0, tiled=True),
        lax.all_to_all(values, "seq", split_axis=1, concat_axis=0, tiled=True),
        lax.all_to_all(out_grad, "seq", split_axis=1, concat_axis=0, tiled=True),
    )
    length = head_q.shape[0]
    heads = head_q.shape[1] // HD
    kv_heads = head_k.shape[1] // HD
    groups = heads // kv_heads
    scale = 1.0 / math.sqrt(HD)
    block = max(512, length // 8)
    starts = list(range(0, length, block))
    query_parts = [[None] * heads for first in starts]
    high = HD
    key_acc = jnp.zeros((length, HD), jnp.float32)
    value_acc = jnp.zeros((length, HD), jnp.float32)
    for number, first in enumerate(starts):
        last = first + block
        query_pos = first + jnp.arange(block)[:, None]
        key_pos = jnp.arange(last)[None, :]
        allowed = key_pos <= query_pos
        key_block = head_k[:last, 0:high]
        value_block = head_v[:last, 0:high]
        for member in range(groups):
            query_block = head_q[first:last, member * HD : (member + 1) * HD]
            grad_block = head_g[first:last, member * HD : (member + 1) * HD]
            scores = (
                lax.dot_general(
                    query_block,
                    key_block,
                    (((1,), (1,)), ((), ())),
                    preferred_element_type=jnp.float32,
                )
                * scale
            )
            scores = jnp.where(allowed, scores, -jnp.inf)
            top = jnp.max(scores, axis=1, keepdims=True)
            expo = jnp.where(allowed, jnp.exp(scores - top), 0.0)
            probs = expo / jnp.sum(expo, axis=1, keepdims=True)
            probs_b = probs.astype(jnp.bfloat16)
            value_acc = value_acc.at[:last].add(
                lax.dot_general(
                    probs_b,
                    grad_block,
                    (((0,), (0,)), ((), ())),
                    preferred_element_type=jnp.float32,
                )
            )
            prob_grad = lax.dot_general(
                grad_block,
                value_block,
                (((1,), (1,)), ((), ())),
                preferred_element_type=jnp.float32,
            )
            delta = jnp.sum(probs * prob_grad, axis=1, keepdims=True)
            score_grad = (probs * (prob_grad - delta) * scale).astype(jnp.bfloat16)
            query_parts[number][member] = jnp.dot(
                score_grad, key_block, preferred_element_type=jnp.float32
            ).astype(jnp.bfloat16)
            key_acc = key_acc.at[:last].add(
                lax.dot_general(
                    score_grad,
                    query_block,
                    (((0,), (0,)), ((), ())),
                    preferred_element_type=jnp.float32,
                )
            )
    key_groups = [key_acc]
    head_query_grad = jnp.concatenate(
        [jnp.concatenate(parts, axis=1) for parts in query_parts], axis=0
    )
    rows_pos = jnp.arange(length)
    key_total = jnp.stack(key_groups, axis=1)
    key_grad = unrotate(key_total, rows_pos).reshape(length, kv_heads * HD).astype(jnp.bfloat16)
    value_grad = value_acc.astype(jnp.bfloat16)
    query_grad = lax.all_to_all(head_query_grad, "seq", split_axis=0, concat_axis=1, tiled=True)
    width = normed.shape[1]
    piece = lax.all_gather(normed, "seq", axis=0, tiled=True)
    key_part = lax.dot_general(
        piece, key_grad, (((0,), (0,)), ((), ())), preferred_element_type=jnp.float32
    )
    value_part = lax.dot_general(
        piece, value_grad, (((0,), (0,)), ((), ())), preferred_element_type=jnp.float32
    )
    key_full, value_full = lax.psum((key_part, value_part), "dp")
    share = width // lax.axis_size("dp")
    offset = lax.axis_index("dp") * share
    key_weight_grad = lax.dynamic_slice_in_dim(key_full, offset, share, 0)
    value_weight_grad = lax.dynamic_slice_in_dim(value_full, offset, share, 0)
    return (query_grad, key_weight_grad, value_weight_grad)


def solution(mesh):
    placed = (
        P(("dp", "seq"), None),
        P(("dp", "seq"), None),
        P(("dp", "seq"), None),
        P(("dp", "seq"), None),
        P(("dp", "seq"), None),
    )
    return jax.shard_map(
        local,
        mesh=mesh,
        in_specs=placed,
        out_specs=(P(("dp", "seq"), None), P("dp", "seq"), P("dp", "seq")),
        check_vma=False,
    )
```

profile of v0, /device:TPU:2, one launch (start us, length us, event | category | flops | bytes accessed | tf_op | source)
XLA Modules:
  0.0 825.3 jit_solution(14754247701670380773)
XLA Ops:
  7.2 1.9 copy.29
  9.1 10.3 %all-to-all-start.1 = ((bf16[128,8,128]{0,2,1:T(8,128)(2,1)}), bf16[128,8,128]{0,2,1:T(8,128)(2,1)S(1)}, u32[]{:S(2)}, u32[]{:S(2)}) async-start(bf16[128,8,128]{0,2,1:T(8,128)(2,1)} %bitcast.3), calls=%async_computation.1 | async-start | bytes 524288 | tf_op jit(solution)/shard_map/all_to_all | solution.py:26
  19.4 1.8 copy.33
  21.1 11.0 %all-to-all-done.1 = bf16[128,8,128]{0,2,1:T(8,128)(2,1)S(1)} async-done(((bf16[128,8,128]{0,2,1:T(8,128)(2,1)}), bf16[128,8,128]{0,2,1:T(8,128)(2,1)S(1)}, u32[]{:S(2)}, u32[]{:S(2)}) %all-to-all-start.1) | async-done | bytes 262176 | tf_op jit(solution)/shard_map/all_to_all | solution.py:26
  32.1 3.4 all-to-all-start.3
  35.6 1.3 copy.27
  36.9 10.7 %all-to-all-done.3 = bf16[128,8,128]{0,2,1:T(8,128)(2,1)S(1)} async-done(((bf16[128,8,128]{0,2,1:T(8,128)(2,1)}), bf16[128,8,128]{0,2,1:T(8,128)(2,1)S(1)}, u32[]{:S(2)}, u32[]{:S(2)}) %all-to-all-start.3) | async-done | bytes 262176 | tf_op jit(solution)/shard_map/all_to_all | solution.py:27
  47.6 3.6 all-to-all-start
  51.1 1.4 copy.31
  52.5 28.0 %all-to-all-done = bf16[128,8,512]{0,2,1:T(8,128)(2,1)S(1)} async-done(((bf16[128,8,512]{0,2,1:T(8,128)(2,1)}), bf16[128,8,512]{0,2,1:T(8,128)(2,1)S(1)}, u32[]{:S(2)}, u32[]{:S(2)}) %all-to-all-start) | async-done | bytes 1048608 | tf_op jit(solution)/shard_map/all_to_all | solution.py:25
  80.5 3.6 all-to-all-start.2
  85.6 0.9 copy.36
  86.6 0.8 copy.34
  87.9 23.6 %all-to-all-done.2 = bf16[128,8,512]{0,2,1:T(8,128)(2,1)S(1)} async-done(((bf16[128,8,512]{0,2,1:T(8,128)(2,1)}), bf16[128,8,512]{0,2,1:T(8,128)(2,1)S(1)}, u32[]{:S(2)}, u32[]{:S(2)}) %all-to-all-start.2) | async-done | bytes 1048608 | tf_op jit(solution)/shard_map/all_to_all | solution.py:28
  121.6 1.8 fusion
  123.4 3.0 fusion.10
  126.4 2.2 multiply_reduce_fusion
  128.7 5.4 multiply_reduce_fusion.3
  134.4 1.3 copy-done.5
  138.3 1.8 fusion.44
  142.0 1.3 convolution_add_fusion.1
  143.3 17.0 %all-gather.2.cloned.1.call-done = bf16[1024,4096]{1,0:T(8,128)(2,1)} async-done(((bf16[128,4096]{1,0:T(8,128)(2,1)}), bf16[1024,4096]{1,0:T(8,128)(2,1)}) %all-gather.2.cloned.1.call-update) | async-done | bytes 8388624 | tf_op jit(solution)/shard_map/all_gather | solution.py:102
  160.3 7.2 convolution_bitcast_fusion
  167.5 6.1 convolution_bitcast_fusion.1
  173.6 1.0 copy-done.9
  178.0 1.2 copy_bitcast_fusion
  179.2 24.3 %all-to-all-start.4 = ((bf16[8,128,512]{1,2,0:T(8,128)(2,1)}), bf16[8,128,512]{1,2,0:T(8,128)(2,1)S(1)}, u32[]{:S(2)}, u32[]{:S(2)}) async-start(bf16[8,128,512]{1,2,0:T(8,128)(2,1)} %copy_bitcast_fusion), calls=%async_computation.4 | async-start | bytes 2097152 | tf_op jit(solution)/shard_map/all_to_all | solution.py:100
  203.5 29.6 %all-to-all-done.4 = bf16[8,128,512]{1,2,0:T(8,128)(2,1)S(1)} async-done(((bf16[8,128,512]{1,2,0:T(8,128)(2,1)}), bf16[8,128,512]{1,2,0:T(8,128)(2,1)S(1)}, u32[]{:S(2)}, u32[]{:S(2)}) %all-to-all-start.4) | async-done | bytes 1048608 | tf_op jit(solution)/shard_map/all_to_all | solution.py:100
  233.1 1.3 copy.38
  234.4 580.8 %all-reduce.5.cloned.1.call-done = (f32[4096,128]{0,1:T(8,128)}, f32[4096,128]{0,1:T(8,128)}) async-done(((f32[4096,128]{0,1:T(8,128)}, f32[4096,128]{0,1:T(8,128)}), (f32[4096,128]{0,1:T(8,128)}, f32[4096,128]{0,1:T(8,128)})) %all-reduce.5.cloned.1.call-update) | async-done | bytes 4194320 | tf_op jit(solution)/shard_map/psum | solution.py:109
  815.2 0.9 constant_dynamic-slice_fusion.1
  816.8 0.9 constant_dynamic-slice_fusion
  (106 shorter events, 21.5 us)
Async XLA Ops:
  7.2 28.4 %copy-start.19 = (bf16[128,4096]{1,0:T(8,128)(2,1)S(1)}, bf16[128,4096]{1,0:T(8,128)(2,1)}, u32[]{:S(2)}) copy-start(bf16[128,4096]{1,0:T(8,128)(2,1)} %param.53) | copy-start | bytes 3145732
  9.1 23.1 %all-to-all-start.1 = ((bf16[128,8,128]{0,2,1:T(8,128)(2,1)}), bf16[128,8,128]{0,2,1:T(8,128)(2,1)S(1)}, u32[]{:S(2)}, u32[]{:S(2)}) async-start(bf16[128,8,128]{0,2,1:T(8,128)(2,1)} %bitcast.3), calls=%async_computation.1 | async-start | bytes 524288 | tf_op jit(solution)/shard_map/all_to_all | solution.py:26
  32.1 15.4 %all-to-all-start.3 = ((bf16[128,8,128]{0,2,1:T(8,128)(2,1)}), bf16[128,8,128]{0,2,1:T(8,128)(2,1)S(1)}, u32[]{:S(2)}, u32[]{:S(2)}) async-start(bf16[128,8,128]{0,2,1:T(8,128)(2,1)} %bitcast.9), calls=%async_computation.3 | async-start | bytes 524288 | tf_op jit(solution)/shard_map/all_to_all | solution.py:27
  35.5 15.6 %copy-start.20 = (bf16[128,4096]{1,0:T(8,128)(2,1)S(1)}, bf16[128,4096]{1,0:T(8,128)(2,1)}, u32[]{:S(2)}) copy-start(bf16[128,4096]{1,0:T(8,128)(2,1)} %param.56) | copy-start | bytes 3145732
  47.6 32.9 %all-to-all-start = ((bf16[128,8,512]{0,2,1:T(8,128)(2,1)}), bf16[128,8,512]{0,2,1:T(8,128)(2,1)S(1)}, u32[]{:S(2)}, u32[]{:S(2)}) async-start(bf16[128,8,512]{0,2,1:T(8,128)(2,1)} %bitcast), calls=%async_computation | async-start | bytes 2097152 | tf_op jit(solution)/shard_map/all_to_all | solution.py:25
  80.5 31.0 %all-to-all-start.2 = ((bf16[128,8,512]{0,2,1:T(8,128)(2,1)}), bf16[128,8,512]{0,2,1:T(8,128)(2,1)S(1)}, u32[]{:S(2)}, u32[]{:S(2)}) async-start(bf16[128,8,512]{0,2,1:T(8,128)(2,1)} %bitcast.6), calls=%async_computation.2 | async-start | bytes 2097152 | tf_op jit(solution)/shard_map/all_to_all | solution.py:28
  84.1 76.2 %all-gather.2.cloned.1.call-start = ((), (), s32[]{:S(2)}) async-start(), calls=%async_computation.5 | async-start | bytes 9437184 | tf_op jit(solution)/shard_map/all_gather | solution.py:102
  84.8 730.4 %all-reduce.5.cloned.1.call-start = ((), (), s32[]{:S(2)}) async-start(), calls=%async_computation.6 | async-start | bytes 8388608 | tf_op jit(solution)/shard_map/psum | solution.py:109
  87.9 33.7 %copy-start.4 = (bf16[8,128,512]{2,1,0:T(8,128)(2,1)}, bf16[8,128,512]{2,1,0:T(8,128)(2,1)S(1)}, u32[]{:S(2)}) copy-start(bf16[8,128,512]{2,1,0:T(8,128)(2,1)S(1)} %copy.28) | copy-start | bytes 3145732
  112.0 5.9 copy-start.16
  112.0 1.0 copy-start.21
  113.7 0.8 copy-start.6
  116.5 0.8 copy-start.10
  117.6 0.8 copy-start.12
  118.6 1.2 copy-start.8
  119.4 1.2 copy-start.17
  119.4 1.3 copy-start.18
  134.1 3.8 copy-start.14
  134.1 1.6 copy-start.5
  136.6 1.0 copy-start
  136.6 1.3 copy-start.2
  137.0 1.3 copy-start.22
  173.6 1.0 copy-start.9
  173.6 1.3 copy-start.13
  173.6 1.6 copy-start.11
  174.6 1.1 copy-start.7
  174.6 1.5 copy-start.15
  174.6 1.9 copy-start.3
  175.2 1.9 copy-start.1
  179.2 53.9 %all-to-all-start.4 = ((bf16[8,128,512]{1,2,0:T(8,128)(2,1)}), bf16[8,128,512]{1,2,0:T(8,128)(2,1)S(1)}, u32[]{:S(2)}, u32[]{:S(2)}) async-start(bf16[8,128,512]{1,2,0:T(8,128)(2,1)} %copy_bitcast_fusion), calls=%async_computation.4 | async-start | bytes 2097152 | tf_op jit(solution)/shard_map/all_to_all | solution.py:100
Sparse Core Ops, SparseCore 0:
  87.0 73.1 all-gather.1
  173.7 641.4 all-reduce.4
where the time goes:
time: 826 us; the launch traced here: 825 us
  waiting for transfers between devices  701 us (85%)
  starting transfers between devices  45.2 us (5%)
  matrix products  36.6 us (4%)
  local copies, waits for them, and re-layouts  18.5 us (2%)
  between operations  14.6 us (2%)
  other arithmetic  9.06 us (1%)
    psum x1, waiting for transfers between devices, local(): key_full, value_full = lax.psum((key_part, value_part), 'dp')  581 us
    all_to_all x1, waiting for transfers between devices, local(): lax.all_to_all(head_query_grad, 'seq', split_axis=0, concat_axis=1, tiled...  29.6 us
    all_to_all x1, waiting for transfers between devices, local(): lax.all_to_all(queries, 'seq', split_axis=1, concat_axis=0, tiled=True)  28 us
    all_to_all x1, starting transfers between devices, local(): lax.all_to_all(head_query_grad, 'seq', split_axis=0, concat_axis=1, tiled...  24.3 us
    all_to_all x1, waiting for transfers between devices, local(): lax.all_to_all(out_grad, 'seq', split_axis=1, concat_axis=0, tiled=True)  23.6 us
    all_gather x1, waiting for transfers between devices, local(): piece = lax.all_gather(normed, 'seq', axis=0, tiled=True)  17 us
  transfers between devices with their start and end apart: 7, of which 7 were waited for; matrix products, arithmetic and copies ran while one was open for 5% of the time, Pallas kernels for 0%

commit v1 on v0

--- a/solution.py
+++ b/solution.py
@@ -99,7 +99,9 @@
     value_grad = value_acc.astype(jnp.bfloat16)
     query_grad = lax.all_to_all(head_query_grad, "seq", split_axis=0, concat_axis=1, tiled=True)
     width = normed.shape[1]
-    piece = lax.all_gather(normed, "seq", axis=0, tiled=True)
+    g_now = jnp.stack([normed for _ in range(lax.axis_size("seq"))], axis=0)
+    answer = lax.all_to_all(g_now, "seq", 0, 0)
+    piece = jnp.concatenate(answer, axis=0)
     key_part = lax.dot_general(
         piece, key_grad, (((0,), (0,)), ((), ())), preferred_element_type=jnp.float32
     )

time: 826 us -> 954 us (1.15)
  waiting for transfers between devices: 701 us -> 811 us
  blocking collectives: 0 us -> 31.6 us
  starting transfers between devices: 45.2 us -> 26.1 us
    all_to_all x1, waiting for transfers between devices: 23.6 us -> 151 us  [local(): answer = lax.all_to_all(g_now, 'seq', 0, 0)]
    all_to_all x0 -> x1, blocking collectives: none -> 31.6 us  [local(): lax.all_to_all(out_grad, 'seq', split_axis=1, concat_axis=0, tiled=True)]
    all_to_all x1, starting transfers between devices: 24.3 us -> 3.56 us  [local(): lax.all_to_all(head_query_grad, 'seq', split_axis=0, concat_axis=1, tiled...]
    all_gather x1 -> x0, waiting for transfers between devices: 17 us -> none  [local(): piece = lax.all_gather(normed, 'seq', axis=0, tiled=True)]
  transfers between devices with their start and end apart: 7 -> 6, of which waited for: 7 -> 6; matrix products, arithmetic and copies ran while one was open for 5% -> 4% of each run, Pallas kernels for 0% -> 0%
where the time goes in v1:
time: 954 us
  waiting for transfers between devices  811 us (85%)
  matrix products  36.5 us (4%)
  blocking collectives  31.6 us (3%)
  starting transfers between devices  26.1 us (3%)
  local copies, waits for them, and re-layouts  24.5 us (3%)
  between operations  14.6 us (2%)
    psum x1, waiting for transfers between devices, local(): key_full, value_full = lax.psum((key_part, value_part), 'dp')  582 us
    all_to_all x1, waiting for transfers between devices, local(): answer = lax.all_to_all(g_now, 'seq', 0, 0)  151 us
    all_to_all x1, blocking collectives, local(): lax.all_to_all(out_grad, 'seq', split_axis=1, concat_axis=0, tiled=True)  31.6 us
    all_to_all x1, waiting for transfers between devices, local(): lax.all_to_all(queries, 'seq', split_axis=1, concat_axis=0, tiled=True)  28.7 us
    all_to_all x1, waiting for transfers between devices, local(): lax.all_to_all(head_query_grad, 'seq', split_axis=0, concat_axis=1, tiled...  27.9 us
  transfers between devices with their start and end apart: 6, of which 6 were waited for; matrix products, arithmetic and copies ran while one was open for 4% of the time, Pallas kernels for 0%

profile of v1, /device:TPU:2, one launch (start us, length us, event | category | flops | bytes accessed | tf_op | source)
XLA Modules:
  0.0 953.5 jit_solution(18110908405676238644)
XLA Ops:
  7.2 1.9 copy.29
  9.1 10.3 %all-to-all-start.1 = ((bf16[128,8,128]{0,2,1:T(8,128)(2,1)}), bf16[128,8,128]{0,2,1:T(8,128)(2,1)S(1)}, u32[]{:S(2)}, u32[]{:S(2)}) async-start(bf16[128,8,128]{0,2,1:T(8,128)(2,1)} %bitcast.3), calls=%async_computation.1 | async-start | bytes 524288 | tf_op jit(solution)/shard_map/all_to_all | solution.py:26
  19.4 1.8 copy.33
  21.1 11.0 %all-to-all-done.1 = bf16[128,8,128]{0,2,1:T(8,128)(2,1)S(1)} async-done(((bf16[128,8,128]{0,2,1:T(8,128)(2,1)}), bf16[128,8,128]{0,2,1:T(8,128)(2,1)S(1)}, u32[]{:S(2)}, u32[]{:S(2)}) %all-to-all-start.1) | async-done | bytes 262176 | tf_op jit(solution)/shard_map/all_to_all | solution.py:26
  32.1 3.4 all-to-all-start.3
  35.6 1.3 copy.27
  36.9 10.7 %all-to-all-done.3 = bf16[128,8,128]{0,2,1:T(8,128)(2,1)S(1)} async-done(((bf16[128,8,128]{0,2,1:T(8,128)(2,1)}), bf16[128,8,128]{0,2,1:T(8,128)(2,1)S(1)}, u32[]{:S(2)}, u32[]{:S(2)}) %all-to-all-start.3) | async-done | bytes 262176 | tf_op jit(solution)/shard_map/all_to_all | solution.py:27
  48.3 3.6 all-to-all-start
  52.5 28.7 %all-to-all-done = bf16[128,8,512]{0,2,1:T(8,128)(2,1)S(1)} async-done(((bf16[128,8,512]{0,2,1:T(8,128)(2,1)}), bf16[128,8,512]{0,2,1:T(8,128)(2,1)S(1)}, u32[]{:S(2)}, u32[]{:S(2)}) %all-to-all-start) | async-done | bytes 1048608 | tf_op jit(solution)/shard_map/all_to_all | solution.py:25
  81.2 31.6 %all_to_all.100 = bf16[128,8,512]{0,2,1:T(8,128)(2,1)S(1)} all-to-all(bf16[128,8,512]{0,2,1:T(8,128)(2,1)S(1)} %bitcast.102), channel_id=1, replica_groups=mesh['dp'=64,'seq'=8] {'seq'}, dimensions={1} | all-to-all | bytes 2097152 | tf_op jit(solution)/shard_map/all_to_all | solution.py:28
  112.7 5.5 stack.5
  118.2 5.1 all-to-all-start.5
  124.3 0.8 copy.36
  125.3 0.8 copy.34
  137.2 1.8 fusion
  139.0 3.0 fusion.10
  142.1 2.2 multiply_reduce_fusion
  144.3 5.4 multiply_reduce_fusion.3
  150.0 1.3 copy-done.5
  153.9 1.8 fusion.51
  157.6 1.3 convolution_add_fusion.1
  158.9 151.1 %all-to-all-done.5 = bf16[8,128,4096]{2,1,0:T(8,128)(2,1)} async-done(((bf16[8,128,4096]{2,1,0:T(8,128)(2,1)}), bf16[8,128,4096]{2,1,0:T(8,128)(2,1)}, u32[]{:S(2)}, u32[]{:S(2)}) %all-to-all-start.5) | async-done | bytes 8388640 | tf_op jit(solution)/shard_map/all_to_all | solution.py:103
  310.0 7.2 convolution_bitcast_fusion
  317.2 6.1 convolution_bitcast_fusion.1
  323.3 1.0 copy-done.9
  327.7 1.2 copy_bitcast_fusion
  328.9 3.6 all-to-all-start.4
  332.5 27.9 %all-to-all-done.4 = bf16[8,128,512]{1,2,0:T(8,128)(2,1)S(1)} async-done(((bf16[8,128,512]{1,2,0:T(8,128)(2,1)}), bf16[8,128,512]{1,2,0:T(8,128)(2,1)S(1)}, u32[]{:S(2)}, u32[]{:S(2)}) %all-to-all-start.4) | async-done | bytes 1048608 | tf_op jit(solution)/shard_map/all_to_all | solution.py:100
  360.4 1.3 copy.38
  361.7 581.8 %all-reduce.5.cloned.1.call-done = (f32[4096,128]{0,1:T(8,128)}, f32[4096,128]{0,1:T(8,128)}) async-done(((f32[4096,128]{0,1:T(8,128)}, f32[4096,128]{0,1:T(8,128)}), (f32[4096,128]{0,1:T(8,128)}, f32[4096,128]{0,1:T(8,128)})) %all-reduce.5.cloned.1.call-update) | async-done | bytes 4194320 | tf_op jit(solution)/shard_map/psum | solution.py:111
  943.4 0.9 constant_dynamic-slice_fusion.1
  944.4 0.9 constant_dynamic-slice_fusion
  (113 shorter events, 22.8 us)
Async XLA Ops:
  7.2 28.4 %copy-start.21 = (bf16[128,4096]{1,0:T(8,128)(2,1)S(1)}, bf16[128,4096]{1,0:T(8,128)(2,1)}, u32[]{:S(2)}) copy-start(bf16[128,4096]{1,0:T(8,128)(2,1)} %param.53) | copy-start | bytes 3145732
  9.1 23.1 %all-to-all-start.1 = ((bf16[128,8,128]{0,2,1:T(8,128)(2,1)}), bf16[128,8,128]{0,2,1:T(8,128)(2,1)S(1)}, u32[]{:S(2)}, u32[]{:S(2)}) async-start(bf16[128,8,128]{0,2,1:T(8,128)(2,1)} %bitcast.3), calls=%async_computation.1 | async-start | bytes 524288 | tf_op jit(solution)/shard_map/all_to_all | solution.py:26
  32.1 15.4 %all-to-all-start.3 = ((bf16[128,8,128]{0,2,1:T(8,128)(2,1)}), bf16[128,8,128]{0,2,1:T(8,128)(2,1)S(1)}, u32[]{:S(2)}, u32[]{:S(2)}) async-start(bf16[128,8,128]{0,2,1:T(8,128)(2,1)} %bitcast.9), calls=%async_computation.3 | async-start | bytes 524288 | tf_op jit(solution)/shard_map/all_to_all | solution.py:27
  35.5 16.3 %copy-start.22 = (bf16[128,4096]{1,0:T(8,128)(2,1)S(1)}, bf16[128,4096]{1,0:T(8,128)(2,1)}, u32[]{:S(2)}) copy-start(bf16[128,4096]{1,0:T(8,128)(2,1)} %param.56) | copy-start | bytes 3145732
  48.3 32.9 %all-to-all-start = ((bf16[128,8,512]{0,2,1:T(8,128)(2,1)}), bf16[128,8,512]{0,2,1:T(8,128)(2,1)S(1)}, u32[]{:S(2)}, u32[]{:S(2)}) async-start(bf16[128,8,512]{0,2,1:T(8,128)(2,1)} %bitcast), calls=%async_computation | async-start | bytes 2097152 | tf_op jit(solution)/shard_map/all_to_all | solution.py:25
  118.2 6.1 copy-start.20
  118.2 191.8 %all-to-all-start.5 = ((bf16[8,128,4096]{2,1,0:T(8,128)(2,1)}), bf16[8,128,4096]{2,1,0:T(8,128)(2,1)}, u32[]{:S(2)}, u32[]{:S(2)}) async-start(bf16[8,128,4096]{2,1,0:T(8,128)(2,1)} %stack.5), calls=%async_computation.5 | async-start | bytes 16777216 | tf_op jit(solution)/shard_map/all_to_all | solution.py:103
  123.3 820.1 %all-reduce.5.cloned.1.call-start = ((), (), s32[]{:S(2)}) async-start(), calls=%async_computation.6 | async-start | bytes 8388608 | tf_op jit(solution)/shard_map/psum | solution.py:111
  126.6 10.6 %copy-start.4 = (bf16[8,128,512]{2,1,0:T(8,128)(2,1)}, bf16[8,128,512]{2,1,0:T(8,128)(2,1)S(1)}, u32[]{:S(2)}) copy-start(bf16[8,128,512]{2,1,0:T(8,128)(2,1)S(1)} %copy.28) | copy-start | bytes 3145732
  127.2 5.9 copy-start.16
  127.6 1.0 copy-start.25
  128.0 0.7 copy-start.23
  129.3 0.9 copy-start.6
  131.7 0.8 copy-start.10
  132.8 0.8 copy-start.12
  133.8 0.8 copy-start.8
  135.1 1.2 copy-start.17
  135.1 1.3 copy-start.18
  149.7 3.9 copy-start.14
  149.7 1.6 copy-start.5
  152.2 1.0 copy-start
  152.2 1.3 copy-start.2
  152.6 1.3 copy-start.26
  152.6 3.2 copy-start.24
  323.3 1.0 copy-start.9
  323.3 1.3 copy-start.13
  323.3 1.6 copy-start.11
  324.4 1.1 copy-start.7
  324.4 1.9 copy-start.3
  324.9 1.8 copy-start.15
  325.8 1.5 copy-start.1
  328.9 31.4 %all-to-all-start.4 = ((bf16[8,128,512]{1,2,0:T(8,128)(2,1)}), bf16[8,128,512]{1,2,0:T(8,128)(2,1)S(1)}, u32[]{:S(2)}, u32[]{:S(2)}) async-start(bf16[8,128,512]{1,2,0:T(8,128)(2,1)} %copy_bitcast_fusion), calls=%async_computation.4 | async-start | bytes 2097152 | tf_op jit(solution)/shard_map/all_to_all | solution.py:100
  (1 other events, 0.7 us)
Sparse Core Ops, SparseCore 0:
  323.5 619.9 all-reduce.4
